TPU v7x, 256 devices: a whole 4x4x8 slice. The times are simulated.
256 devices in a mesh: seq: 32 (over y, z), head: 8 (over x, core).
Axes of the slice: x: 4, y: 4, z: 8, core: 2. Of those that a mesh axis runs over, the one named last changes fastest.
Arguments:
- new_query: bfloat16 [96, 4, 4096], P(None, None, 'head'), may hold values from -40 to 40
- fresh_key_value: bfloat16 [96, 4, 8, 128], P('seq', None, 'head'), may hold values from -24 to 24
- prompt_cache: bfloat16 [8, 32768, 8, 128], P(None, 'seq', 'head'), may hold values from -30 to 30
- decoded_tail_cache: bfloat16 [96, 1024, 8, 128], P(None, 'seq', 'head'), may hold values from -6 to 6
- sinks: float32 [64], P('head'), may hold values from 2 to 14
- prompt_group: int32 [96], replicated, may hold values from 0 to 7, as said below
- prompt_lens: int32 [8], replicated, may hold values from 1 to 32768
- tail_lens: int32 [96], replicated, may hold values from 0 to 1024
- o_weight: bfloat16 [4096, 2880], P('head'), may hold values from -0.09375 to 0.09375
- resid: bfloat16 [96, 4, 2880], P('seq'), may hold values from -1.796875 to 1.796875
- norm_gain: float32 [2880], replicated, may hold values from 0.3 to 3
- expert_ids: int32 [96, 4, 4], replicated, may hold values from 0 to 31, all different within a row; in each aligned block of 12 rows (0 to 11, 12 to 23, ..., all dimensions but the last counted through in order) at most 3 rows name the same one
- route_weights: float32 [96, 4, 4], P('seq'), may hold values from 0.05 to 0.6
- gate_up: bfloat16 [32, 2880, 2, 2880], P('seq', None, None, 'head'), may hold values from -0.3125 to 0.3125
- down_weight: bfloat16 [32, 2880, 2880], P('seq', 'head'), may hold values from -0.0390625 to 0.0390625
Outputs:
- output: bfloat16 [96, 4, 2880], P('seq')
Inputs may be any that keep to these rules, and one draw needn't show every extreme that they name: `prompt_group`: each of the 8 groups holds exactly 12 requests. `expert_ids`: a token's 4 picks are distinct; among the 12 tokens of the requests s * 3 to (s + 1) * 3 - 1 no expert is picked more than 3 times.
All inputs are finite; a program needn't handle non-finite values.
Results may differ from a plain program's by a relative error of at most 0.025.
Values may be sent and summed in bfloat16 or wider, within the bound.
A program may use at most 128 MiB of HBM per device.

v0:
```python
import math
import jax
import jax.numpy as jnp
from jax import lax
from jax.sharding import PartitionSpec as P

very_low = -1e30


def rotate(vector, position):
    half_width = vector.shape[-1] // 2
    frequency = jnp.exp(
        jnp.arange(half_width, dtype=jnp.float32) * (-2.0 * math.log(150000.0) / vector.shape[-1])
    )
    angle = position[..., None] * frequency
    cosine = jnp.cos(angle)
    sine_part = jnp.sin(angle)
    leading = vector[..., :half_width]
    trailing = vector[..., half_width:]
    return jnp.concatenate(
        [leading * cosine - trailing * sine_part, trailing * cosine + leading * sine_part], axis=-1
    )


def block_weights(scores, valid):
    masked = jnp.where(valid, scores, very_low)
    highest = jnp.max(masked, axis=-1)
    weights = jnp.where(valid, jnp.exp(masked - highest[..., None]), 0.0)
    return (highest, jnp.sum(weights, axis=-1), weights)


def joined_stats(first, second):
    highest_a, total_a, weighted_a = first
    highest_b, total_b, weighted_b = second
    highest = jnp.maximum(highest_a, highest_b)
    factor_a = jnp.exp(highest_a - highest)
    factor_b = jnp.exp(highest_b - highest)
    spread_count = weighted_a.shape[-1] // highest_a.shape[-1]
    weighted = weighted_a * jnp.repeat(factor_a, spread_count, axis=-1) + weighted_b * jnp.repeat(
        factor_b, spread_count, axis=-1
    )
    return (highest, total_a * factor_a + total_b * factor_b, weighted)


def slot_numbers(picks, experts_total):
    one_hot = (picks[..., None] == jnp.arange(experts_total, dtype=jnp.int32)).astype(jnp.int32)
    earlier = jnp.cumsum(one_hot, axis=-2) - one_hot
    return jnp.sum(earlier * one_hot, axis=-1)


def on_device(
    new_query,
    fresh_key_value,
    prompt_cache,
    decoded_tail_cache,
    sinks,
    prompt_group,
    prompt_lens,
    tail_lens,
    o_weight,
    resid,
    norm_gain,
    expert_ids,
    route_weights,
    gate_up,
    down_weight,
):
    seq_count = lax.axis_size("seq")
    seq_index = lax.axis_index("seq")
    groups_total, prompt_block, kv_local, double_width = prompt_cache.shape
    head_dim = double_width // 2
    requests, steps_total, query_width = new_query.shape
    heads_local = query_width // head_dim
    requests_per_group = heads_local // kv_local
    owned = fresh_key_value.shape[0]
    tail_block = decoded_tail_cache.shape[1]
    group_size = requests // groups_total
    model_width = resid.shape[-1]
    factor_scale = 1.0 / math.sqrt(head_dim)
    first_row = seq_index * owned
    group_hot = prompt_group[:, None] == jnp.arange(groups_total, dtype=jnp.int32)[None, :]
    prompt_start = jnp.sum(jnp.where(group_hot, prompt_lens[None, :], 0), axis=1)
    positions = (
        (prompt_start + tail_lens)[:, None] + jnp.arange(steps_total, dtype=jnp.int32)[None, :]
    ).astype(jnp.float32)
    query_matrix = new_query.reshape(requests, steps_total, heads_local, head_dim).astype(
        jnp.float32
    )
    rotated = rotate(query_matrix, positions[:, :, None]).astype(jnp.bfloat16)
    rotated = rotated.reshape(requests, steps_total, kv_local, requests_per_group, head_dim)
    ordering = jnp.argsort(prompt_group, stable=True)
    inverse = jnp.zeros_like(ordering).at[ordering].set(jnp.arange(requests, dtype=jnp.int32))
    grouped = rotated[ordering].reshape(
        groups_total, group_size, steps_total, kv_local, requests_per_group, head_dim
    )
    prompt_scores = (
        jnp.einsum(
            "grtcjd,gpcd->grtcjp",
            grouped,
            prompt_cache[..., :head_dim],
            preferred_element_type=jnp.float32,
        )
        * factor_scale
    )
    prompt_valid = (seq_index * prompt_block + jnp.arange(prompt_block, dtype=jnp.int32))[
        None, :
    ] < prompt_lens[:, None]
    prompt_high, prompt_total, prompt_weights = block_weights(
        prompt_scores, prompt_valid[:, None, None, None, None, :]
    )
    prompt_acc = jnp.einsum(
        "grtcjp,gpcd->grtcjd",
        prompt_weights.astype(jnp.bfloat16),
        prompt_cache[..., head_dim:],
        preferred_element_type=jnp.float32,
    )
    prompt_stats = (
        prompt_high.reshape(requests, steps_total, heads_local)[inverse],
        prompt_total.reshape(requests, steps_total, heads_local)[inverse],
        prompt_acc.reshape(requests, steps_total, query_width)[inverse],
    )
    tail_scores = (
        jnp.einsum(
            "rtcjd,rucd->rtcju",
            rotated,
            decoded_tail_cache[..., :head_dim],
            preferred_element_type=jnp.float32,
        )
        * factor_scale
    )
    tail_valid = (seq_index * tail_block + jnp.arange(tail_block, dtype=jnp.int32))[
        None, :
    ] < tail_lens[:, None]
    tail_high, tail_total, tail_weights = block_weights(
        tail_scores, tail_valid[:, None, None, None, :]
    )
    tail_acc = jnp.einsum(
        "rtcju,rucd->rtcjd",
        tail_weights.astype(jnp.bfloat16),
        decoded_tail_cache[..., head_dim:],
        preferred_element_type=jnp.float32,
    )
    tail_stats = (
        tail_high.reshape(requests, steps_total, heads_local),
        tail_total.reshape(requests, steps_total, heads_local),
        tail_acc.reshape(requests, steps_total, query_width),
    )
    local_stats = joined_stats(prompt_stats, tail_stats)
    own_query = lax.dynamic_slice_in_dim(rotated, first_row, owned, 0)
    own_positions = lax.dynamic_slice_in_dim(positions, first_row, owned, 0)
    fresh_keys = rotate(
        fresh_key_value[..., :head_dim].astype(jnp.float32), own_positions[:, :, None]
    ).astype(jnp.bfloat16)
    fresh_scores = (
        jnp.einsum("rtcjd,rucd->rtcju", own_query, fresh_keys, preferred_element_type=jnp.float32)
        * factor_scale
    )
    causal = jnp.arange(steps_total)[None, :] <= jnp.arange(steps_total)[:, None]
    fresh_high, fresh_total, fresh_weights = block_weights(
        fresh_scores, causal[None, :, None, None, :]
    )
    fresh_acc = jnp.einsum(
        "rtcju,rucd->rtcjd",
        fresh_weights.astype(jnp.bfloat16),
        fresh_key_value[..., head_dim:],
        preferred_element_type=jnp.float32,
    )
    fresh_stats = (
        fresh_high.reshape(owned, steps_total, heads_local),
        fresh_total.reshape(owned, steps_total, heads_local),
        fresh_acc.reshape(owned, steps_total, query_width),
    )
    by_owner = tuple(
        (member.reshape((seq_count, owned) + member.shape[1:]) for member in local_stats)
    )
    recv_high, recv_total, recv_acc = (
        lax.all_to_all(by_owner[0], "seq", split_axis=0, concat_axis=0, tiled=True),
        lax.all_to_all(by_owner[1], "seq", split_axis=0, concat_axis=0, tiled=True),
        lax.all_to_all(by_owner[2], "seq", split_axis=0, concat_axis=0, tiled=True),
    )
    owner_high = jnp.max(recv_high, axis=0)
    factors = jnp.exp(recv_high - owner_high[None])
    owner_total = jnp.sum(recv_total * factors, axis=0)
    owner_acc = jnp.sum(recv_acc * jnp.repeat(factors, head_dim, axis=-1), axis=0)
    final_stats = joined_stats((owner_high, owner_total, owner_acc), fresh_stats)
    final_high, final_total, final_acc = final_stats
    with_sink = jnp.maximum(final_high, sinks)
    kept = jnp.exp(final_high - with_sink)
    denom_total = final_total * kept + jnp.exp(sinks - with_sink)
    attended = (final_acc * jnp.repeat(kept / denom_total, head_dim, axis=-1)).astype(jnp.bfloat16)
    token_count = owned * steps_total
    partial_proj = jnp.dot(
        attended.reshape(token_count, query_width), o_weight, preferred_element_type=jnp.float32
    )
    projected = lax.psum(partial_proj, "head")
    hidden = (resid.reshape(token_count, model_width).astype(jnp.float32) + projected).astype(
        jnp.bfloat16
    )
    wide = hidden.astype(jnp.float32)
    normed = (
        wide * lax.rsqrt(jnp.mean(wide * wide, axis=-1, keepdims=True) + 1e-05) * norm_gain
    ).astype(jnp.bfloat16)
    experts_local = gate_up.shape[0]
    hidden_local = gate_up.shape[-1]
    experts_total = experts_local * seq_count
    top_count = expert_ids.shape[-1]
    capacity = token_count * top_count // experts_total + 2
    pair_count = token_count * top_count
    all_picks = expert_ids.reshape(seq_count, pair_count)
    own_picks = lax.dynamic_slice_in_dim(all_picks, seq_index, 1, 0)[0]
    own_index = own_picks * capacity + slot_numbers(own_picks, experts_total)
    pair_token = jnp.arange(pair_count, dtype=jnp.int32) // top_count
    joined_weight = gate_up.reshape(experts_local, model_width, 2 * hidden_local)
    outgoing = (
        jnp.zeros((experts_total * capacity, model_width), jnp.bfloat16)
        .at[own_index]
        .set(normed[pair_token])
    )
    outgoing = outgoing.reshape(seq_count, experts_local, capacity, model_width)
    projected_rows = jnp.einsum(
        "nekd,edf->nekf",
        lax.all_to_all(outgoing, "seq", split_axis=0, concat_axis=0, tiled=True),
        joined_weight,
        preferred_element_type=jnp.float32,
    )
    gate_part = jnp.minimum(projected_rows[..., :hidden_local], 7.0)
    up_part = jnp.clip(projected_rows[..., hidden_local:], -7.0, 7.0)
    activation = ((up_part + 1.0) * gate_part * jax.nn.sigmoid(1.702 * gate_part)).astype(
        jnp.bfloat16
    )
    returned = lax.all_to_all(
        jnp.einsum("nekf,efd->nekd", activation, down_weight, preferred_element_type=jnp.float32),
        "seq",
        split_axis=0,
        concat_axis=0,
        tiled=True,
    )
    back_rows = returned.reshape(experts_total * capacity, model_width)[own_index]
    weighted = back_rows.reshape(token_count, top_count, model_width) * route_weights.reshape(
        token_count, top_count, 1
    )
    expert_part = jnp.sum(weighted, axis=1)
    expert_total = lax.psum(expert_part, "head")
    return (wide + expert_total).astype(jnp.bfloat16).reshape(owned, steps_total, model_width)


def solution(mesh):
    return jax.shard_map(
        on_device,
        mesh=mesh,
        in_specs=(
            P(None, None, "head"),
            P("seq", None, "head", None),
            P(None, "seq", "head", None),
            P(None, "seq", "head", None),
            P("head"),
            P(),
            P(),
            P(),
            P("head", None),
            P("seq", None, None),
            P(),
            P(),
            P("seq", None, None),
            P("seq", None, None, "head"),
            P("seq", "head", None),
        ),
        out_specs=P("seq", None, None),
        check_vma=False,
    )
```

profile of v0, /device:TPU:8, one launch (start us, length us, event | category | flops | bytes accessed | tf_op | source)
XLA Modules:
  0.0 368.7 jit_solution(5805711957272378757)
XLA Ops:
  7.5 3.2 sort.17
  16.9 3.4 copy.153
  20.3 2.3 copy.154
  24.2 2.4 add_convert_fusion
  29.1 2.7 gather_fusion
  31.8 3.7 %fusion.1 = (f32[8,12,4,8]{3,2,1,0:T(4,128)S(1)}, f32[8,12,4,8,1024]{4,3,2,1,0:T(8,128)S(1)}) fusion(pred[8,1024]{1,0:T(8,128)(4,1)S(1)} %broadcast_compare_fusion.1, bf16[8,12,4,8,64]{4,3,2,1,0:T(8,128)(2,1)} %bitcast.215, bf16[8,1024,1,128]{3,1,2,0:T(8,128)(2,1)} %param.17), kind=kOutput, calls=%fused_computation.11 | convolution fusion | flops 412087296 | bytes 15093760 | tf_op jit(solution)/shard_map/grtcjd,gpcd->grtcjp/dot_general | solution.py:97
  35.6 4.0 %fusion.2 = f32[8,12,4,8]{3,2,1,0:T(4,128)S(1)} fusion(f32[8,12,4,8,1024]{4,3,2,1,0:T(8,128)S(1)} %get-tuple-element.29, f32[8,12,4,8]{3,2,1,0:T(4,128)S(1)} %get-tuple-element.28, pred[8,1024]{1,0:T(8,128)(4,1)S(1)} %broadcast_compare_fusion.1), kind=kLoop, calls=%fused_computation.12 | loop fusion | flops 15725568 | bytes 12615680 | tf_op jit(solution)/shard_map/reduce_sum | solution.py:29
  42.2 2.6 fusion.98
  48.0 11.8 %all-to-all-start.2 = ((f32[32,3,4,8]{3,2,1,0:T(4,128)}), f32[32,3,4,8]{3,2,1,0:T(4,128)}, u32[]{:S(2)}, u32[]{:S(2)}) async-start(f32[32,3,4,8]{3,2,1,0:T(4,128)} %get-tuple-element.11), calls=%async_computation.2 | async-start | bytes 393216 | tf_op jit(solution)/shard_map/all_to_all | solution.py:178
  60.5 3.8 %convolution_bitcast_fusion.1 = f32[96,4,1,8,64]{4,3,1,0,2:T(8,128)} fusion(f32[96,4,1,8,32]{4,3,1,0,2:T(8,128)} %copy-done.4, bf16[96,32,1,128]{3,1,0,2:T(8,128)(2,1)} %bitcast.224, f32[96,4,8]{2,1,0:T(4,128)S(1)} %get-tuple-element.26, pred[96,32]{1,0:T(8,128)(4,1)} %broadcast_compare_fusion), kind=kOutput, calls=%fused_computation.30 | convolution fusion | flops 12877824 | bytes 1981440 | tf_op jit(solution)/shard_map/rtcju,rucd->rtcjd/dot_general | solution.py:137
  65.0 9.5 %fusion.16 = f32[8,12,4,1,8,64]{5,4,2,1,0,3:T(8,128)} fusion(bf16[8,1024,1,128]{3,1,2,0:T(8,128)(2,1)} %param.17, f32[8,12,4,8,1024]{4,3,2,1,0:T(8,128)} %copy-done.1, f32[8,12,4,8]{3,2,1,0:T(4,128)S(1)} %get-tuple-element.28, pred[8,1024]{1,0:T(8,128)(4,1)S(1)} %broadcast_compare_fusion.1), kind=kOutput, calls=%fused_computation.31 | convolution fusion | flops 418381824 | bytes 15679488 | tf_op jit(solution)/shard_map/grtcjp,gpcd->grtcjd/dot_general | solution.py:111
  75.4 2.7 reshape.441
  78.4 2.7 reshape.435
  81.1 3.2 gather_fusion.1
  85.9 2.7 reshape.442
  90.2 2.7 reshape.438
  92.9 3.2 multiply_add_fusion
  96.1 9.8 %all-to-all-start.1 = ((f32[32,3,4,8]{3,2,1,0:T(4,128)}), f32[32,3,4,8]{3,2,1,0:T(4,128)S(1)}, u32[]{:S(2)}, u32[]{:S(2)}) async-start(f32[32,3,4,8]{3,2,1,0:T(4,128)} %get-tuple-element.12), calls=%async_computation.1 | async-start | bytes 393216 | tf_op jit(solution)/shard_map/all_to_all | solution.py:177
  106.6 9.0 %all-to-all-done.1 = f32[32,3,4,8]{3,2,1,0:T(4,128)S(1)} async-done(((f32[32,3,4,8]{3,2,1,0:T(4,128)}), f32[32,3,4,8]{3,2,1,0:T(4,128)S(1)}, u32[]{:S(2)}, u32[]{:S(2)}) %all-to-all-start.1) | async-done | bytes 12320 | tf_op jit(solution)/shard_map/all_to_all | solution.py:177
  115.5 5.7 %all-to-all-start = ((f32[32,3,4,512]{3,2,1,0:T(4,128)}), f32[32,3,4,512]{3,2,1,0:T(4,128)}, u32[]{:S(2)}, u32[]{:S(2)}) async-start(f32[32,3,4,512]{3,2,1,0:T(4,128)} %multiply_add_fusion), calls=%async_computation | async-start | bytes 1572864 | tf_op jit(solution)/shard_map/all_to_all | solution.py:179
  129.8 2.7 reshape.444
  132.5 7.3 %all-to-all-done = f32[32,3,4,512]{3,2,1,0:T(4,128)} async-done(((f32[32,3,4,512]{3,2,1,0:T(4,128)}), f32[32,3,4,512]{3,2,1,0:T(4,128)}, u32[]{:S(2)}, u32[]{:S(2)}) %all-to-all-start) | async-done | bytes 786464 | tf_op jit(solution)/shard_map/all_to_all | solution.py:179
  143.1 63.7 %all-reduce.3.cloned.1.call-done = f32[12,2880]{1,0:T(8,128)} async-done(((f32[12,2880]{1,0:T(8,128)}), f32[12,2880]{1,0:T(8,128)}) %all-reduce.3.cloned.1.call-update) | async-done | bytes 138256 | tf_op jit(solution)/shard_map/psum | solution.py:195
  209.2 2.9 scatter_custom_fusion.1
  213.2 27.5 %all_to_all.25 = bf16[32,1,3,2880]{3,2,1,0:T(4,128)(2,1)S(1)} all-to-all(bf16[32,1,3,2880]{3,2,1,0:T(4,128)(2,1)} %bitcast.220), channel_id=1, replica_groups=mesh['seq'=32,'head'=8] {'seq'}, dimensions={0} | all-to-all | bytes 1105920 | tf_op jit(solution)/shard_map/all_to_all | solution.py:222
  240.7 3.7 %convolution_bitcast_fusion.2 = f32[32,1,3,720]{3,0,2,1:T(8,128)S(1)} fusion(bf16[2880,720,1]{0,1,2:T(8,128)(2,1)} %bitcast.217, bf16[32,1,3,2880]{3,2,1,0:T(4,128)(2,1)S(1)} %all_to_all.25), kind=kOutput, calls=%fused_computation.34 | convolution fusion | flops 398131200 | bytes 4976640 | tf_op jit(solution)/shard_map/nekd,edf->nekf/dot_general | solution.py:220
  247.2 7.7 %all-to-all-start.4 = ((f32[32,1,3,2880]{3,1,2,0:T(1,128)}), f32[32,1,3,2880]{3,1,2,0:T(1,128)}, u32[]{:S(2)}, u32[]{:S(2)}) async-start(f32[32,1,3,2880]{3,1,2,0:T(1,128)} %copy.142), calls=%async_computation.4 | async-start | bytes 2260992 | tf_op jit(solution)/shard_map/all_to_all | solution.py:231
  255.3 24.7 %all-to-all-done.4 = f32[32,1,3,2880]{3,1,2,0:T(1,128)} async-done(((f32[32,1,3,2880]{3,1,2,0:T(1,128)}), f32[32,1,3,2880]{3,1,2,0:T(1,128)}, u32[]{:S(2)}, u32[]{:S(2)}) %all-to-all-start.4) | async-done | bytes 1105952 | tf_op jit(solution)/shard_map/all_to_all | solution.py:231
  280.0 5.5 %reduce.6 = f32[32,3,2880]{2,1,0:T(4,128)} reduce(f32[32,1,3,2880]{3,1,2,0:T(1,128)} %all-to-all-done.4, f32[]{:T(128)} %constant.78), dimensions={1}, to_apply=%all_to_all.19.reduce_sub_computation | reduce | bytes 2211844 | tf_op jit(solution)/shard_map/all_to_all | solution.py:231
  285.5 2.7 reshape.459
  288.1 3.0 gather_fusion.4
  293.5 66.7 %all-reduce.5.cloned.1.call-done = f32[12,2880]{1,0:T(8,128)} async-done(((f32[12,2880]{1,0:T(8,128)}), f32[12,2880]{1,0:T(8,128)}) %all-reduce.5.cloned.1.call-update) | async-done | bytes 138256 | tf_op jit(solution)/shard_map/psum | solution.py:243
  (132 shorter events, 45.9 us)
Async XLA Ops:
  6.5 134.9 %copy-start = (bf16[512,2880]{0,1:T(8,128)(2,1)S(1)}, bf16[512,2880]{0,1:T(8,128)(2,1)}, u32[]{:S(2)}) copy-start(bf16[512,2880]{0,1:T(8,128)(2,1)} %param.23) | copy-start | bytes 8847364
  6.5 16.0 %copy-start.24 = (f32[32]{0:T(128)}, f32[32]{0:T(128)S(1)}, u32[]{:S(2)}) copy-start(f32[32]{0:T(128)S(1)} %multiply_exponential_fusion) | copy-start | bytes 388
  11.6 29.2 %copy-start.19 = (s32[1024]{0:T(1024)}, s32[1024]{0:T(1024)S(1)}, u32[]{:S(2)}) copy-start(s32[1024]{0:T(1024)S(1)} %pad_clamp_fusion.2) | copy-start | bytes 12292
  14.4 8.2 %copy-start.9 = (f32[96,4]{1,0:T(8,128)}, f32[96,4]{1,0:T(8,128)S(1)}, u32[]{:S(2)}) copy-start(f32[96,4]{1,0:T(8,128)S(1)} %add_convert_fusion.2) | copy-start | bytes 4612
  16.9 3.4 copy-start.6
  26.7 0.9 copy-start.2
  26.7 1.1 copy-start.3
  35.5 4.6 %copy-start.1 = (f32[8,12,4,8,1024]{4,3,2,1,0:T(8,128)}, f32[8,12,4,8,1024]{4,3,2,1,0:T(8,128)S(1)}, u32[]{:S(2)}) copy-start(f32[8,12,4,8,1024]{4,3,2,1,0:T(8,128)S(1)} %get-tuple-element.29) | copy-start | bytes 37748740
  42.2 3.8 %copy-start.11 = (pred[96,32]{1,0:T(8,128)(4,1)S(1)}, pred[96,32]{1,0:T(8,128)(4,1)}, u32[]{:S(2)}) copy-start(pred[96,32]{1,0:T(8,128)(4,1)} %broadcast_compare_fusion) | copy-start | bytes 9220
  42.2 4.9 %copy-start.8 = (f32[96,4,8]{2,1,0:T(4,128)S(1)}, f32[96,4,8]{2,1,0:T(4,128)}, u32[]{:S(2)}) copy-start(f32[96,4,8]{2,1,0:T(4,128)} %gather_fusion.3) | copy-start | bytes 36868
  44.9 1.1 copy-start.4
  48.0 48.0 %all-to-all-start.2 = ((f32[32,3,4,8]{3,2,1,0:T(4,128)}), f32[32,3,4,8]{3,2,1,0:T(4,128)}, u32[]{:S(2)}, u32[]{:S(2)}) async-start(f32[32,3,4,8]{3,2,1,0:T(4,128)} %get-tuple-element.11), calls=%async_computation.2 | async-start | bytes 393216 | tf_op jit(solution)/shard_map/all_to_all | solution.py:178
  65.0 9.5 %copy-start.18 = (s32[96,4,4]{0,2,1:T(4,128)S(1)}, s32[96,4,4]{0,2,1:T(4,128)}, u32[]{:S(2)}) copy-start(s32[96,4,4]{0,2,1:T(4,128)} %param.26) | copy-start | bytes 18436
  74.5 3.6 copy-start.13
  74.5 3.6 copy-start.14
  74.8 3.4 copy-start.21
  92.9 3.2 copy-start.17
  92.9 28.6 %copy-start.25 = (f32[32]{0:T(128)S(1)}, f32[32]{0:T(128)}, u32[]{:S(2)}) copy-start(f32[32]{0:T(128)} %copy-done.24) | copy-start | bytes 388
  92.9 28.8 %copy-start.12 = (bf16[3,4,2880]{2,1,0:T(4,128)(2,1)S(1)}, bf16[3,4,2880]{2,1,0:T(4,128)(2,1)}, u32[]{:S(2)}) copy-start(bf16[3,4,2880]{2,1,0:T(4,128)(2,1)} %param.24) | copy-start | bytes 207364
  96.0 28.3 %copy-start.22 = (s32[48]{0:T(128)S(1)}, s32[48]{0:T(128)}, u32[]{:S(2)}) copy-start(s32[48]{0:T(128)} %copy-done.21) | copy-start | bytes 580
  96.1 19.5 %all-to-all-start.1 = ((f32[32,3,4,8]{3,2,1,0:T(4,128)}), f32[32,3,4,8]{3,2,1,0:T(4,128)S(1)}, u32[]{:S(2)}, u32[]{:S(2)}) async-start(f32[32,3,4,8]{3,2,1,0:T(4,128)} %get-tuple-element.12), calls=%async_computation.1 | async-start | bytes 393216 | tf_op jit(solution)/shard_map/all_to_all | solution.py:177
  115.5 24.3 %all-to-all-start = ((f32[32,3,4,512]{3,2,1,0:T(4,128)}), f32[32,3,4,512]{3,2,1,0:T(4,128)}, u32[]{:S(2)}, u32[]{:S(2)}) async-start(f32[32,3,4,512]{3,2,1,0:T(4,128)} %multiply_add_fusion), calls=%async_computation | async-start | bytes 1572864 | tf_op jit(solution)/shard_map/all_to_all | solution.py:179
  121.2 85.6 %all-reduce.3.cloned.1.call-start = ((), (), s32[]{:S(2)}) async-start(), calls=%async_computation.5 | async-start | bytes 376832 | tf_op jit(solution)/shard_map/psum | solution.py:195
  129.8 11.7 %copy-start.10 = (f32[12,512]{1,0:T(8,128)S(1)}, f32[12,512]{1,0:T(8,128)}, u32[]{:S(2)}) copy-start(f32[12,512]{1,0:T(8,128)} %reshape.448) | copy-start | bytes 73732
  141.4 1.7 copy-start.26
  141.4 67.1 %copy-start.16 = (f32[2880]{0:T(1024)S(1)}, f32[2880]{0:T(1024)}, u32[]{:S(2)}) copy-start(f32[2880]{0:T(1024)} %param.25) | copy-start | bytes 34564
  141.5 67.7 %copy-start.23 = (s32[48]{0:T(128)S(1)}, s32[48]{0:T(128)}, u32[]{:S(2)}) copy-start(s32[48]{0:T(128)} %fusion.82) | copy-start | bytes 580
  207.8 0.6 copy-start.7
  240.7 3.8 %copy-start.5 = (bf16[1,360,2880]{2,1,0:T(8,128)(2,1)S(1)}, bf16[1,360,2880]{2,1,0:T(8,128)(2,1)}, u32[]{:S(2)}) copy-start(bf16[1,360,2880]{2,1,0:T(8,128)(2,1)} %param.29) | copy-start | bytes 6220804
  245.0 10.2 %copy-start.20 = (f32[3,4,4]{2,1,0:T(4,128)S(1)}, f32[3,4,4]{2,1,0:T(4,128)}, u32[]{:S(2)}) copy-start(f32[3,4,4]{2,1,0:T(4,128)} %param.27) | copy-start | bytes 580
  247.2 32.8 %all-to-all-start.4 = ((f32[32,1,3,2880]{3,1,2,0:T(1,128)}), f32[32,1,3,2880]{3,1,2,0:T(1,128)}, u32[]{:S(2)}, u32[]{:S(2)}) async-start(f32[32,1,3,2880]{3,1,2,0:T(1,128)} %copy.142), calls=%async_computation.4 | async-start | bytes 2260992 | tf_op jit(solution)/shard_map/all_to_all | solution.py:231
  254.9 105.2 %all-reduce.5.cloned.1.call-start = ((), (), s32[]{:S(2)}) async-start(), calls=%async_computation.6 | async-start | bytes 376832 | tf_op jit(solution)/shard_map/psum | solution.py:243
  (1 other events, 0.6 us)
Sparse Core Ops, SparseCore 0:
  143.2 63.5 all-reduce.2
  293.6 66.4 all-reduce.4
where the time goes:
time: 370 us; the launch traced here: 369 us
  waiting for transfers between devices  171 us (46%)
  local copies, waits for them, and re-layouts  57 us (15%)
  other arithmetic  36.6 us (10%)
  starting transfers between devices  35.5 us (10%)
  blocking collectives  27.5 us (7%)
  matrix products  26.8 us (7%)
  between operations  13.9 us (4%)
    psum x1, waiting for transfers between devices, on_device(): expert_total = lax.psum(expert_part, 'head')  66.7 us
    psum x1, waiting for transfers between devices, on_device(): projected = lax.psum(partial_proj, 'head')  63.7 us
    all_to_all x1, blocking collectives, on_device(): lax.all_to_all(outgoing, 'seq', split_axis=0, concat_axis=0, tiled=True)  27.5 us
    all_to_all x1, waiting for transfers between devices, on_device(): lax.all_to_all(jnp.einsum('nekf,efd->nekd', activation, down_weight, pref...  24.7 us
    all_to_all x1, starting transfers between devices, on_device(): lax.all_to_all(by_owner[1], 'seq', split_axis=0, concat_axis=0, tiled=True)  11.8 us
    unnamed x58, local copies, waits for them, and re-layouts  11.2 us
    all_to_all x1, starting transfers between devices, on_device(): lax.all_to_all(by_owner[0], 'seq', split_axis=0, concat_axis=0, tiled=True)  9.79 us
    dot_general x1, matrix products, on_device(): jnp.einsum('grtcjp,gpcd->grtcjd', prompt_weights.astype(jnp.bfloat16), pr...  9.51 us
  transfers between devices with their start and end apart: 6, of which 5 were waited for; matrix products, arithmetic and copies ran while one was open for 13% of the time, Pallas kernels for 0%

commit v1 on v0

--- a/solution.py
+++ b/solution.py
@@ -192,7 +192,7 @@
     partial_proj = jnp.dot(
         attended.reshape(token_count, query_width), o_weight, preferred_element_type=jnp.float32
     )
-    projected = lax.psum(partial_proj, "head")
+    projected = jnp.sum(lax.all_gather(partial_proj, "head"), axis=0)
     hidden = (resid.reshape(token_count, model_width).astype(jnp.float32) + projected).astype(
         jnp.bfloat16
     )

time: 370 us -> 330 us (0.89)
  waiting for transfers between devices: 171 us -> 131 us
    psum x1 -> x0, waiting for transfers between devices: 63.7 us -> none  [on_device(): projected = lax.psum(partial_proj, 'head')]
    all_gather x0 -> x1, waiting for transfers between devices: none -> 24.6 us  [on_device(): projected = jnp.sum(lax.all_gather(partial_proj, 'head'), axis=0)]
    psum x1, waiting for transfers between devices: 66.7 us -> 62.5 us  [on_device(): expert_total = lax.psum(expert_part, 'head')]
    unnamed x58 -> x38, local copies, waits for them, and re-layouts: 11.2 us -> 10.1 us
where the time goes in v1:
time: 330 us; the launch traced here: 328 us
  waiting for transfers between devices  131 us (40%)
  local copies, waits for them, and re-layouts  54.8 us (17%)
  other arithmetic  35.9 us (11%)
  starting transfers between devices  35.3 us (11%)
  blocking collectives  30.5 us (9%)
  matrix products  26.8 us (8%)
  between operations  13.8 us (4%)
    psum x1, waiting for transfers between devices, on_device(): expert_total = lax.psum(expert_part, 'head')  62.5 us
    all_to_all x1, blocking collectives, on_device(): lax.all_to_all(outgoing, 'seq', split_axis=0, concat_axis=0, tiled=True)  30.5 us
    all_to_all x1, waiting for transfers between devices, on_device(): lax.all_to_all(jnp.einsum('nekf,efd->nekd', activation, down_weight, pref...  27.2 us
    all_gather x1, waiting for transfers between devices, on_device(): projected = jnp.sum(lax.all_gather(partial_proj, 'head'), axis=0)  24.6 us
    all_to_all x1, starting transfers between devices, on_device(): lax.all_to_all(by_owner[1], 'seq', split_axis=0, concat_axis=0, tiled=True)  11.8 us
    unnamed x38, local copies, waits for them, and re-layouts  10.1 us
    all_to_all x1, waiting for transfers between devices, on_device(): lax.all_to_all(by_owner[2], 'seq', split_axis=0, concat_axis=0, tiled=True)  9.98 us
    all_to_all x1, starting transfers between devices, on_device(): lax.all_to_all(by_owner[0], 'seq', split_axis=0, concat_axis=0, tiled=True)  9.78 us
  transfers between devices with their start and end apart: 6, of which 5 were waited for; matrix products, arithmetic and copies ran while one was open for 13% of the time, Pallas kernels for 0%

profile of v1, /device:TPU:8, one launch (start us, length us, event | category | flops | bytes accessed | tf_op | source)
XLA Modules:
  0.0 328.1 jit_solution(16924144192745075541)
XLA Ops:
  7.5 3.2 sort.17
  16.9 3.4 %copy.153 = f32[96,4,8,32]{3,2,1,0:T(8,128)} copy(f32[96,4,8,32]{0,3,2,1:T(8,128)} %get-tuple-element.15) | data formatting | bytes 786432
  20.3 2.3 copy.154
  24.2 2.4 add_convert_fusion
  29.1 2.7 gather_fusion
  31.8 3.7 %fusion.1 = (f32[8,12,4,8]{3,2,1,0:T(4,128)S(1)}, f32[8,12,4,8,1024]{4,3,2,1,0:T(8,128)S(1)}) fusion(pred[8,1024]{1,0:T(8,128)(4,1)S(1)} %broadcast_compare_fusion.1, bf16[8,12,4,8,64]{4,3,2,1,0:T(8,128)(2,1)} %bitcast.217, bf16[8,1024,1,128]{3,1,2,0:T(8,128)(2,1)} %param.17), kind=kOutput, calls=%fused_computation.11 | convolution fusion | flops 412087296 | bytes 15093760 | tf_op jit(solution)/shard_map/grtcjd,gpcd->grtcjp/dot_general | solution.py:97
  35.5 4.0 %fusion.2 = f32[8,12,4,8]{3,2,1,0:T(4,128)S(1)} fusion(f32[8,12,4,8,1024]{4,3,2,1,0:T(8,128)S(1)} %get-tuple-element.29, f32[8,12,4,8]{3,2,1,0:T(4,128)S(1)} %get-tuple-element.28, pred[8,1024]{1,0:T(8,128)(4,1)S(1)} %broadcast_compare_fusion.1), kind=kLoop, calls=%fused_computation.12 | loop fusion | flops 15725568 | bytes 12615680 | tf_op jit(solution)/shard_map/reduce_sum | solution.py:29
  42.2 2.6 fusion.96
  48.0 11.8 %all-to-all-start.2 = ((f32[32,3,4,8]{3,2,1,0:T(4,128)}), f32[32,3,4,8]{3,2,1,0:T(4,128)}, u32[]{:S(2)}, u32[]{:S(2)}) async-start(f32[32,3,4,8]{3,2,1,0:T(4,128)} %get-tuple-element.11), calls=%async_computation.2 | async-start | bytes 393216 | tf_op jit(solution)/shard_map/all_to_all | solution.py:178
  60.5 3.7 %convolution_bitcast_fusion.2 = f32[96,4,1,8,64]{4,3,1,0,2:T(8,128)} fusion(f32[96,4,1,8,32]{4,3,1,0,2:T(8,128)} %copy-done.4, bf16[96,32,1,128]{3,1,0,2:T(8,128)(2,1)} %bitcast.226, f32[96,4,8]{2,1,0:T(4,128)S(1)} %get-tuple-element.26, pred[96,32]{1,0:T(8,128)(4,1)} %broadcast_compare_fusion), kind=kOutput, calls=%fused_computation.31 | convolution fusion | flops 12877824 | bytes 1981440 | tf_op jit(solution)/shard_map/rtcju,rucd->rtcjd/dot_general | solution.py:137
  64.3 9.6 %fusion.16 = f32[8,12,4,1,8,64]{5,4,2,1,0,3:T(8,128)} fusion(bf16[8,1024,1,128]{3,1,2,0:T(8,128)(2,1)} %param.17, f32[8,12,4,8,1024]{4,3,2,1,0:T(8,128)} %copy-done.1, f32[8,12,4,8]{3,2,1,0:T(4,128)S(1)} %get-tuple-element.28, pred[8,1024]{1,0:T(8,128)(4,1)S(1)} %broadcast_compare_fusion.1), kind=kOutput, calls=%fused_computation.32 | convolution fusion | flops 418381824 | bytes 15679488 | tf_op jit(solution)/shard_map/grtcjp,gpcd->grtcjd/dot_general | solution.py:111
  73.9 2.7 reshape.451
  76.9 2.7 reshape.445
  79.6 3.0 gather_fusion.1
  84.2 2.7 reshape.452
  88.5 2.7 reshape.448
  91.2 9.8 %all-to-all-start.1 = ((f32[32,3,4,8]{3,2,1,0:T(4,128)}), f32[32,3,4,8]{3,2,1,0:T(4,128)S(1)}, u32[]{:S(2)}, u32[]{:S(2)}) async-start(f32[32,3,4,8]{3,2,1,0:T(4,128)} %get-tuple-element.12), calls=%async_computation.1 | async-start | bytes 393216 | tf_op jit(solution)/shard_map/all_to_all | solution.py:177
  101.0 3.1 multiply_add_fusion
  104.2 6.5 %all-to-all-done.1 = f32[32,3,4,8]{3,2,1,0:T(4,128)S(1)} async-done(((f32[32,3,4,8]{3,2,1,0:T(4,128)}), f32[32,3,4,8]{3,2,1,0:T(4,128)S(1)}, u32[]{:S(2)}, u32[]{:S(2)}) %all-to-all-start.1) | async-done | bytes 12320 | tf_op jit(solution)/shard_map/all_to_all | solution.py:177
  110.7 5.7 %all-to-all-start = ((f32[32,3,4,512]{3,2,1,0:T(4,128)}), f32[32,3,4,512]{3,2,1,0:T(4,128)}, u32[]{:S(2)}, u32[]{:S(2)}) async-start(f32[32,3,4,512]{3,2,1,0:T(4,128)} %multiply_add_fusion), calls=%async_computation | async-start | bytes 1572864 | tf_op jit(solution)/shard_map/all_to_all | solution.py:179
  122.3 2.7 reshape.454
  125.0 10.0 %all-to-all-done = f32[32,3,4,512]{3,2,1,0:T(4,128)} async-done(((f32[32,3,4,512]{3,2,1,0:T(4,128)}), f32[32,3,4,512]{3,2,1,0:T(4,128)}, u32[]{:S(2)}, u32[]{:S(2)}) %all-to-all-start) | async-done | bytes 786464 | tf_op jit(solution)/shard_map/all_to_all | solution.py:179
  139.4 24.6 %all-gather.4.cloned.1.call-done = f32[8,12,2880]{2,1,0:T(8,128)} async-done(((f32[1,12,2880]{2,1,0:T(8,128)}), f32[8,12,2880]{2,1,0:T(8,128)}) %all-gather.4.cloned.1.call-update) | async-done | bytes 1105936 | tf_op jit(solution)/shard_map/all_gather | solution.py:195
  167.3 3.0 scatter_custom_fusion.1
  171.4 30.5 %all_to_all.25 = bf16[32,1,3,2880]{3,2,1,0:T(4,128)(2,1)S(1)} all-to-all(bf16[32,1,3,2880]{3,2,1,0:T(4,128)(2,1)} %bitcast.222), channel_id=1, replica_groups=mesh['seq'=32,'head'=8] {'seq'}, dimensions={0} | all-to-all | bytes 1105920 | tf_op jit(solution)/shard_map/all_to_all | solution.py:222
  201.9 3.7 %convolution_bitcast_fusion.3 = f32[32,1,3,720]{3,0,2,1:T(8,128)S(1)} fusion(bf16[2880,720,1]{0,1,2:T(8,128)(2,1)} %bitcast.219, bf16[32,1,3,2880]{3,2,1,0:T(4,128)(2,1)S(1)} %all_to_all.25), kind=kOutput, calls=%fused_computation.35 | convolution fusion | flops 398131200 | bytes 4976640 | tf_op jit(solution)/shard_map/nekd,edf->nekf/dot_general | solution.py:220
  208.4 7.5 %all-to-all-start.4 = ((f32[32,1,3,2880]{3,1,2,0:T(1,128)}), f32[32,1,3,2880]{3,1,2,0:T(1,128)}, u32[]{:S(2)}, u32[]{:S(2)}) async-start(f32[32,1,3,2880]{3,1,2,0:T(1,128)} %copy.142), calls=%async_computation.4 | async-start | bytes 2260992 | tf_op jit(solution)/shard_map/all_to_all | solution.py:231
  216.3 27.2 %all-to-all-done.4 = f32[32,1,3,2880]{3,1,2,0:T(1,128)} async-done(((f32[32,1,3,2880]{3,1,2,0:T(1,128)}), f32[32,1,3,2880]{3,1,2,0:T(1,128)}, u32[]{:S(2)}, u32[]{:S(2)}) %all-to-all-start.4) | async-done | bytes 1105952 | tf_op jit(solution)/shard_map/all_to_all | solution.py:231
  243.5 5.5 %reduce.8 = f32[32,3,2880]{2,1,0:T(4,128)} reduce(f32[32,1,3,2880]{3,1,2,0:T(1,128)} %all-to-all-done.4, f32[]{:T(128)} %constant.78), dimensions={1}, to_apply=%all_to_all.19.reduce_sub_computation | reduce | bytes 2211844 | tf_op jit(solution)/shard_map/all_to_all | solution.py:231
  249.0 2.7 reshape.469
  251.7 3.0 gather_fusion.4
  257.1 62.5 %all-reduce.2.cloned.1.call-done = f32[12,2880]{1,0:T(8,128)} async-done(((f32[12,2880]{1,0:T(8,128)}), f32[12,2880]{1,0:T(8,128)}) %all-reduce.2.cloned.1.call-update) | async-done | bytes 138256 | tf_op jit(solution)/shard_map/psum | solution.py:243
  (115 shorter events, 43.0 us)
Async XLA Ops:
  6.5 130.1 %copy-start = (bf16[512,2880]{0,1:T(8,128)(2,1)S(1)}, bf16[512,2880]{0,1:T(8,128)(2,1)}, u32[]{:S(2)}) copy-start(bf16[512,2880]{0,1:T(8,128)(2,1)} %param.23) | copy-start | bytes 8847364
  14.4 8.2 %copy-start.9 = (f32[96,4]{1,0:T(8,128)}, f32[96,4]{1,0:T(8,128)S(1)}, u32[]{:S(2)}) copy-start(f32[96,4]{1,0:T(8,128)S(1)} %add_convert_fusion.3) | copy-start | bytes 4612
  16.9 3.4 %copy-start.6 = (f32[96,4,8,32]{0,3,2,1:T(8,128)S(1)}, f32[96,4,8,32]{0,3,2,1:T(8,128)}, u32[]{:S(2)}) copy-start(f32[96,4,8,32]{0,3,2,1:T(8,128)} %get-tuple-element.16) | copy-start | bytes 1179652
  26.6 0.9 copy-start.2
  26.6 1.1 copy-start.3
  35.5 4.6 %copy-start.1 = (f32[8,12,4,8,1024]{4,3,2,1,0:T(8,128)}, f32[8,12,4,8,1024]{4,3,2,1,0:T(8,128)S(1)}, u32[]{:S(2)}) copy-start(f32[8,12,4,8,1024]{4,3,2,1,0:T(8,128)S(1)} %get-tuple-element.29) | copy-start | bytes 37748740
  42.2 3.8 %copy-start.10 = (pred[96,32]{1,0:T(8,128)(4,1)S(1)}, pred[96,32]{1,0:T(8,128)(4,1)}, u32[]{:S(2)}) copy-start(pred[96,32]{1,0:T(8,128)(4,1)} %broadcast_compare_fusion) | copy-start | bytes 9220
  42.2 5.0 %copy-start.7 = (f32[96,4,8]{2,1,0:T(4,128)S(1)}, f32[96,4,8]{2,1,0:T(4,128)}, u32[]{:S(2)}) copy-start(f32[96,4,8]{2,1,0:T(4,128)} %gather_fusion.3) | copy-start | bytes 36868
  44.8 1.2 copy-start.4
  48.0 43.2 %all-to-all-start.2 = ((f32[32,3,4,8]{3,2,1,0:T(4,128)}), f32[32,3,4,8]{3,2,1,0:T(4,128)}, u32[]{:S(2)}, u32[]{:S(2)}) async-start(f32[32,3,4,8]{3,2,1,0:T(4,128)} %get-tuple-element.11), calls=%async_computation.2 | async-start | bytes 393216 | tf_op jit(solution)/shard_map/all_to_all | solution.py:178
  64.3 9.6 %copy-start.11 = (f32[96,4,8]{0,2,1:T(8,128)S(1)}, f32[96,4,8]{0,2,1:T(8,128)}, u32[]{:S(2)}) copy-start(f32[96,4,8]{0,2,1:T(8,128)} %copy.131) | copy-start | bytes 36868
  91.2 19.5 %all-to-all-start.1 = ((f32[32,3,4,8]{3,2,1,0:T(4,128)}), f32[32,3,4,8]{3,2,1,0:T(4,128)S(1)}, u32[]{:S(2)}, u32[]{:S(2)}) async-start(f32[32,3,4,8]{3,2,1,0:T(4,128)} %get-tuple-element.12), calls=%async_computation.1 | async-start | bytes 393216 | tf_op jit(solution)/shard_map/all_to_all | solution.py:177
  101.0 16.4 %copy-start.12 = (bf16[3,4,1,128]{3,1,2,0:T(4,128)(2,1)S(1)}, bf16[3,4,1,128]{3,1,2,0:T(4,128)(2,1)}, u32[]{:S(2)}) copy-start(bf16[3,4,1,128]{3,1,2,0:T(4,128)(2,1)} %param.16) | copy-start | bytes 9220
  104.2 16.0 %copy-start.16 = (f32[8]{0:T(128)S(1)}, f32[8]{0:T(128)}, u32[]{:S(2)}) copy-start(f32[8]{0:T(128)} %param.19) | copy-start | bytes 100
  110.7 24.3 %all-to-all-start = ((f32[32,3,4,512]{3,2,1,0:T(4,128)}), f32[32,3,4,512]{3,2,1,0:T(4,128)}, u32[]{:S(2)}, u32[]{:S(2)}) async-start(f32[32,3,4,512]{3,2,1,0:T(4,128)} %multiply_add_fusion), calls=%async_computation | async-start | bytes 1572864 | tf_op jit(solution)/shard_map/all_to_all | solution.py:179
  116.4 47.7 %all-gather.4.cloned.1.call-start = ((), (), s32[]{:S(2)}) async-start(), calls=%async_computation.6 | async-start | bytes 1695744 | tf_op jit(solution)/shard_map/all_gather | solution.py:195
  136.6 1.6 copy-start.8
  136.6 1.7 copy-start.13
  201.9 3.8 %copy-start.5 = (bf16[1,360,2880]{2,1,0:T(8,128)(2,1)S(1)}, bf16[1,360,2880]{2,1,0:T(8,128)(2,1)}, u32[]{:S(2)}) copy-start(bf16[1,360,2880]{2,1,0:T(8,128)(2,1)} %param.29) | copy-start | bytes 6220804
  206.2 10.0 %copy-start.14 = (f32[3,4,4]{2,1,0:T(4,128)S(1)}, f32[3,4,4]{2,1,0:T(4,128)}, u32[]{:S(2)}) copy-start(f32[3,4,4]{2,1,0:T(4,128)} %param.27) | copy-start | bytes 580
  206.2 10.0 %copy-start.15 = (s32[48]{0:T(128)S(1)}, s32[48]{0:T(128)}, u32[]{:S(2)}) copy-start(s32[48]{0:T(128)} %fusion.80) | copy-start | bytes 580
  208.4 35.1 %all-to-all-start.4 = ((f32[32,1,3,2880]{3,1,2,0:T(1,128)}), f32[32,1,3,2880]{3,1,2,0:T(1,128)}, u32[]{:S(2)}, u32[]{:S(2)}) async-start(f32[32,1,3,2880]{3,1,2,0:T(1,128)} %copy.142), calls=%async_computation.4 | async-start | bytes 2260992 | tf_op jit(solution)/shard_map/all_to_all | solution.py:231
  215.9 103.6 %all-reduce.2.cloned.1.call-start = ((), (), s32[]{:S(2)}) async-start(), calls=%async_computation.5 | async-start | bytes 376832 | tf_op jit(solution)/shard_map/psum | solution.py:243
Sparse Core Ops, SparseCore 0:
  138.3 25.7 all-gather.3
  257.2 62.3 all-reduce.1
